TPU v7x, 128 devices: a whole 4x4x4 slice. The times are simulated.
128 devices in a mesh: seq: 16 (over y, z), batch: 8 (over x, core).
Axes of the slice: x: 4, y: 4, z: 4, core: 2. Of those that a mesh axis runs over, the one named last changes fastest.
Arguments:
- q_nope: bfloat16 [8, 64, 128, 128], P('batch', None, 'seq'), may hold values from -6 to 6
- q_rope: bfloat16 [8, 64, 128, 64], P('batch', None, 'seq'), may hold values from -8 to 8
- absorb_k: bfloat16 [128, 128, 512], P('seq'), may hold values from -0.5 to 0.5
- absorb_v: bfloat16 [128, 512, 128], P('seq'), may hold values from -0.25 to 0.25
- cache_latent: bfloat16 [8, 16384, 512], P('batch', 'seq'), may hold values from -6 to 6
- cache_rope: bfloat16 [8, 16384, 64], P('batch', 'seq'), may hold values from -8 to 8
- draft_latent: bfloat16 [8, 64, 512], P('batch'), may hold values from -6 to 6
- draft_rope: bfloat16 [8, 64, 64], P('batch'), may hold values from -6 to 6
- residual: bfloat16 [512, 7168], P('batch', 'seq'), may hold values from -1.2 to 1.2
- out_proj: bfloat16 [16384, 7168], P('seq'), may hold values from -0.046875 to 0.046875
- norm_gain: float32 [7168], replicated, may hold values from 0.5 to 1.5
- lm_head: bfloat16 [65536, 7168], P(('seq', 'batch')), may hold values from -2.4095235 to 2.4095235
- parent: int32 [8, 64], replicated, may hold values from 0 to 62, as said below
- draft_ids: int32 [8, 64], replicated, may hold values from 0 to 65535
- cache_len: int32 [8], P('batch'), may hold values from 4096 to 16384
- accept_len: int32 [8], P('batch'), may hold values from 1 to 64
Outputs:
- hidden_out: bfloat16 [512, 7168], P('batch', 'seq')
- target_logp: float32 [8, 64], P('batch')
- accepted_score: float32 [8], P('batch')
Inputs may be any that keep to these rules, and one draw needn't show every extreme that they name: parent[b, 0] = 0, and 0 <= parent[b, i] < i for i >= 1.
All inputs are finite; a program needn't handle non-finite values.
Results may differ from a plain program's by a relative error of at most 0.0095.
Values may be sent and summed in bfloat16 or wider, within the bound.
A program may use at most 256 MiB of HBM per device.

v0:
```python
import math
import jax
import jax.numpy as jnp
from jax import lax
from jax.sharding import Mesh
from jax.sharding import PartitionSpec as P

SEQ = ("seq_0", "seq_1")
BATCH = ("batch_0", "batch_1")
SEQ_BATCH = ("seq_0", "seq_1", "batch_0", "batch_1")
masked_value = -1e30
norm_epsilon = 1e-06
highest = lax.Precision.HIGHEST


def sent_together(arrays, axis, dim, along):
    ends, at = ([], 0)
    for a in arrays[:-1]:
        at += a.shape[along]
        ends.append(at)
    both = jnp.concatenate(arrays, axis=along)
    return tuple(jnp.split(lax.all_gather(both, axis, axis=dim, tiled=True), ends, axis=along))


def copy_for_each(array, axis):
    copies = jnp.broadcast_to(array, (lax.axis_size(axis), *array.shape))
    return lax.all_to_all(copies, axis, split_axis=0, concat_axis=0, tiled=True)


def over_copies(array, axis):
    everything = copy_for_each(array, axis)
    return jnp.max(everything, axis=0)


def gathered_once(array, axis):
    leaves = jax.tree.leaves(array)
    sequence = sorted(range(len(leaves)), key=lambda k: -leaves[k].size)
    width = (1, *leaves[sequence[0]].shape)[-1]
    lines = [
        jnp.pad(leaves[k].reshape(-1), (0, -leaves[k].size % width)).reshape(-1, width)
        for k in sequence
    ]
    both, at, found = (lax.all_gather(jnp.concatenate(lines), axis), 0, {})
    for k, line in zip(sequence, lines):
        piece = both[:, at : at + len(line)].reshape(len(both), -1)
        found[k] = piece[:, : leaves[k].size].reshape(-1, *leaves[k].shape)
        at += len(line)
    numbers = iter(range(len(leaves)))
    return jax.tree.map(lambda _: found[next(numbers)], array)


def combined_by_axis(array, axes, combine):
    for axis in axes:
        pieces = gathered_once(array, axis)
        array = jax.tree.map(lambda part: part[0], pieces)
        for k in range(1, lax.axis_size(axis)):
            array = combine(array, jax.tree.map(lambda part: part[k], pieces))
    return array


def ancestry_of(parents):
    draft_count = parents.shape[1]
    indices = jnp.arange(draft_count, dtype=jnp.int32)
    parent_map = (
        (parents[:, :, None] == indices[None, None, :]) & (indices[None, :, None] > 0)
    ).astype(jnp.float32)
    ancestry = jnp.broadcast_to(jnp.eye(draft_count, dtype=jnp.float32), parent_map.shape)
    for doubling in range(draft_count.bit_length() - 1):
        ancestry = ancestry + jnp.einsum("rij,rjk->rik", ancestry, parent_map, precision=highest)
        parent_map = jnp.einsum("rij,rjk->rik", parent_map, parent_map, precision=highest)
    return ancestry > 0.5


def combine_soft(earlier, later):
    top_new = jnp.maximum(earlier[0], later[0])
    mass_new = earlier[1] * jnp.exp(earlier[0] - top_new) + later[1] * jnp.exp(later[0] - top_new)
    return (top_new, mass_new, earlier[2] + later[2])


def body(
    q_nope,
    q_rope,
    absorb_k,
    absorb_v,
    cache_latent,
    cache_rope,
    draft_latent,
    draft_rope,
    residual,
    out_proj,
    norm_gain,
    lm_head,
    parent,
    draft_ids,
    cache_len,
    accept_len,
):
    requests, draft_count, local_heads, nope_width = q_nope.shape
    cache_rows = cache_latent.shape[1]
    score_scale = 1.0 / math.sqrt(nope_width + q_rope.shape[3])
    seq_index = lax.axis_index(SEQ)
    batch_index = lax.axis_index(BATCH)
    query_latent = jnp.einsum(
        "rihn,hnc->rihc", q_nope, absorb_k, preferred_element_type=jnp.float32
    ).astype(jnp.bfloat16)
    query_all, rope_all = sent_together((query_latent, q_rope), SEQ, 2, 3)
    cache_scores = jnp.einsum(
        "rihc,rtc->rhit", query_all, cache_latent, preferred_element_type=jnp.float32
    )
    cache_scores = cache_scores + jnp.einsum(
        "rihe,rte->rhit", rope_all, cache_rope, preferred_element_type=jnp.float32
    )
    positions = seq_index * cache_rows + jnp.arange(cache_rows, dtype=jnp.int32)
    in_cache = positions[None, :] < cache_len[:, None]
    cache_scores = jnp.where(in_cache[:, None, None, :], cache_scores * score_scale, masked_value)
    tree_scores = jnp.einsum(
        "rihc,rjc->rhij", query_all, draft_latent, preferred_element_type=jnp.float32
    )
    tree_scores = tree_scores + jnp.einsum(
        "rihe,rje->rhij", rope_all, draft_rope, preferred_element_type=jnp.float32
    )
    own_parents = lax.dynamic_slice_in_dim(parent, batch_index * requests, requests, 0)
    ancestry = ancestry_of(own_parents)
    tree_scores = jnp.where(ancestry[:, None, :, :], tree_scores * score_scale, masked_value)
    local_top = jnp.maximum(jnp.max(cache_scores, axis=3), jnp.max(tree_scores, axis=3))
    row_top = over_copies(local_top, SEQ)
    cache_weights = jnp.exp(cache_scores - row_top[..., None])
    weight_sum = jnp.sum(cache_weights, axis=3)
    partial_value = jnp.einsum(
        "rhit,rtc->rhic",
        cache_weights.astype(jnp.bfloat16),
        cache_latent,
        preferred_element_type=jnp.float32,
    )
    head_first = seq_index * local_heads
    tree_mine = lax.dynamic_slice_in_dim(tree_scores, head_first, local_heads, 1)
    top_mine = lax.dynamic_slice_in_dim(row_top, head_first, local_heads, 1)
    tree_weights = jnp.exp(tree_mine - top_mine[..., None])
    tree_out = jnp.einsum(
        "rhij,rjc->rhic",
        tree_weights.astype(jnp.bfloat16),
        draft_latent,
        preferred_element_type=jnp.float32,
    )
    latent_sum, weight_total = (
        lax.psum_scatter(partial_value, SEQ, scatter_dimension=1, tiled=True),
        lax.psum_scatter(weight_sum, SEQ, scatter_dimension=1, tiled=True),
    )
    summed = jnp.einsum(
        "rhic,hcn->rhin", latent_sum + tree_out, absorb_v, preferred_element_type=jnp.float32
    )
    weight_total = weight_total + jnp.sum(tree_weights, axis=3)
    head_out = (summed / weight_total[..., None]).astype(jnp.bfloat16)
    head_rows = jnp.transpose(head_out, (0, 2, 1, 3)).reshape(
        requests * draft_count, local_heads * head_out.shape[3]
    )
    branch_term = jnp.dot(head_rows, out_proj, preferred_element_type=jnp.float32)
    width_local = residual.shape[1]
    feature_first = seq_index * width_local
    residual_wide = lax.dynamic_update_slice_in_dim(
        jnp.zeros_like(branch_term), residual.astype(jnp.float32), feature_first, 1
    )
    stream = lax.psum(branch_term + residual_wide, SEQ)
    square = jnp.sum(stream * stream, axis=1)
    normed = (
        stream * lax.rsqrt(square / stream.shape[1] + norm_epsilon)[:, None] * norm_gain
    ).astype(jnp.bfloat16)
    hidden_out = lax.dynamic_slice_in_dim(stream, feature_first, width_local, 1).astype(
        jnp.bfloat16
    )
    vocab_rows = lm_head.shape[0]
    vocab_first = lax.axis_index(SEQ_BATCH) * vocab_rows
    logits = jnp.einsum(
        "rd,vd->rv",
        lax.all_gather(normed, BATCH, axis=0, tiled=True),
        lm_head,
        preferred_element_type=jnp.float32,
    )
    request_total = parent.shape[0]
    parent_rows = (
        jnp.arange(request_total, dtype=jnp.int32)[:, None] * draft_count + parent
    ).reshape(-1)
    source = logits[parent_rows]
    column = jnp.arange(vocab_rows, dtype=jnp.int32) + vocab_first
    picked = jnp.sum(
        jnp.where(column[None, :] == draft_ids.reshape(-1)[:, None], source, 0.0), axis=1
    )
    local_best = jnp.max(logits, axis=1)
    local_mass = jnp.sum(jnp.exp(logits - local_best[:, None]), axis=1)
    best, exp_mass, chosen = combined_by_axis(
        (local_best, local_mass, picked), SEQ_BATCH, combine_soft
    )
    log_total = best + jnp.log(exp_mass)
    target_all = (chosen - log_total[parent_rows]).reshape(request_total, draft_count)
    target_logp = lax.dynamic_slice_in_dim(target_all, batch_index * requests, requests, 0)
    accepted_score = jnp.sum(
        jnp.where(
            jnp.arange(draft_count, dtype=jnp.int32)[None, :] < accept_len[:, None],
            target_logp,
            0.0,
        ),
        axis=1,
    )
    return (hidden_out, target_logp, accepted_score)


def solution(mesh):
    split = Mesh(mesh.devices.reshape(4, 4, 4, 2), ("seq_0", "seq_1", "batch_0", "batch_1"))
    in_specs = (
        P(BATCH, None, SEQ, None),
        P(BATCH, None, SEQ, None),
        P(SEQ, None, None),
        P(SEQ, None, None),
        P(BATCH, SEQ, None),
        P(BATCH, SEQ, None),
        P(BATCH, None, None),
        P(BATCH, None, None),
        P(BATCH, SEQ),
        P(SEQ, None),
        P(),
        P(SEQ_BATCH, None),
        P(),
        P(),
        P(BATCH),
        P(BATCH),
    )
    out_specs = (P(BATCH, SEQ), P(BATCH, None), P(BATCH))
    return jax.shard_map(body, mesh=split, in_specs=in_specs, out_specs=out_specs, check_vma=False)
```

profile of v0, /device:TPU:1, one launch (start us, length us, event | category | flops | bytes accessed | tf_op | source)
XLA Modules:
  0.0 529.6 jit_solution(17929896783594325636)
XLA Ops:
  7.2 1.0 copy.41
  8.2 1.6 fusion.16
  9.9 0.9 maximum_bitcast_fusion
  11.5 0.7 fusion.88
  12.2 0.2 fusion.39
  12.5 0.2 convolution_add_fusion.5
  12.7 0.2 fusion.99
  12.8 0.2 convolution_add_fusion.4
  13.0 0.2 fusion.100
  13.2 0.2 convolution_add_fusion.3
  13.3 0.2 fusion.101
  13.5 0.2 convolution_add_fusion.2
  13.7 0.2 fusion.102
  13.9 0.2 convolution_add_fusion.1
  14.0 0.2 fusion.17
  14.2 0.1 copy.45
  14.3 80.4 %all-gather.11.cloned.1.call-done = bf16[1,64,128,576]{3,1,0,2:T(8,128)(2,1)} async-done(((bf16[1,64,8,576]{3,1,0,2:T(8,128)(2,1)}), bf16[1,64,128,576]{3,1,0,2:T(8,128)(2,1)}) %all-gather.11.cloned.1.call-update) | async-done | bytes 9437200 | tf_op jit(solution)/shard_map/all_gather | solution.py:22
  94.7 1.8 split.9
  96.5 2.9 copy.69
  99.4 7.5 %fusion.10 = f32[64,128,64]{0,2,1:T(8,128)S(1)} fusion(bf16[1,64,512]{2,1,0:T(8,128)(2,1)S(1)} %copy-done.5, bf16[1,64,128,576]{3,1,0,2:T(8,128)(2,1)} %all-gather.11.cloned.1.call-done), kind=kOutput, calls=%fused_computation.11 | convolution fusion | flops 536870912 | bytes 10551296 | tf_op jit(solution)/shard_map/rihc,rjc->rhij/dot_general | solution.py:116
  106.9 5.8 %fusion.97 = (f32[128,64]{1,0:T(8,128)S(1)}, f32[1,128,64,64]{2,3,1,0:T(8,128)}) fusion(f32[64,128,64]{0,2,1:T(8,128)S(1)} %fusion.10, bf16[1,64,64]{2,1,0:T(8,128)(2,1)S(1)} %copy-done.8, bf16[1,64,128,576]{3,1,0,2:T(8,128)(2,1)} %all-gather.11.cloned.1.call-done, pred[64,64]{0,1:T(8,128)(4,1)S(1)} %copy.45), kind=kOutput, calls=%fused_computation.169 | convolution fusion | flops 69197824 | bytes 6336512 | tf_op jit(solution)/shard_map/rihe,rje->rhij/dot_general | solution.py:119
  112.8 7.7 %split.8 = bf16[1,64,128,512]{3,1,0,2:T(8,128)(2,1)} slice(bf16[1,64,128,576]{3,1,0,2:T(8,128)(2,1)} %all-gather.11.cloned.1.call-done), slice={[0:1], [0:64], [0:128], [0:512]} | slice | bytes 16777216 | tf_op jit(solution)/shard_map/split | solution.py:22
  120.5 30.0 %fusion.12 = f32[64,128,1024]{2,1,0:T(8,128)} fusion(bf16[1,64,128,512]{3,1,0,2:T(8,128)(2,1)} %split.8, bf16[1,1024,512]{2,1,0:T(8,128)(2,1)S(1)} %copy-done), kind=kOutput, calls=%fused_computation.14 | convolution fusion | flops 8589934592 | bytes 42991616 | tf_op jit(solution)/shard_map/rihc,rtc->rhit/dot_general | solution.py:107
  150.5 21.9 %fusion.96 = (f32[128,64]{0,1:T(8,128)S(1)}, f32[1,128,64,1024]{3,1,2,0:T(8,128)}) fusion(f32[64,128,1024]{2,1,0:T(8,128)} %fusion.12, bf16[1,1024,64]{1,2,0:T(8,128)(2,1)S(1)} %copy-done.4, bf16[1,64,128,64]{2,3,1,0:T(8,128)(2,1)S(1)} %copy-done.3, pred[1024]{0:T(1024)(128)(4,1)S(1)} %add_compare_fusion), kind=kOutput, calls=%fused_computation.168 | convolution fusion | flops 1107288064 | bytes 68322304 | tf_op jit(solution)/shard_map/rihe,rte->rhit/dot_general | solution.py:110
  172.5 15.1 %all_to_all.5 = f32[16,1,128,64]{2,3,1,0:T(8,128)S(1)} all-to-all(f32[16,1,128,64]{2,3,1,0:T(8,128)S(1)} %broadcast_in_dim.37), channel_id=1, replica_groups=mesh['seq_0'=4,'seq_1'=4,'batch_0'=4,'batch_1'=2] {'seq_0','seq_1'}, dimensions={0} | all-to-all | bytes 1048576 | tf_op jit(solution)/shard_map/all_to_all | solution.py:27
  187.7 18.7 %fusion.7 = f32[1,128,64,512]{3,1,2,0:T(8,128)} fusion(f32[1,128,64,1024]{3,1,2,0:T(8,128)} %get-tuple-element.19, f32[128,64]{0,1:T(8,128)S(1)} %reduce_max.38, bf16[1,1024,512]{2,1,0:T(8,128)(2,1)S(1)} %copy-done), kind=kOutput, calls=%fused_computation.10 | convolution fusion | flops 8606711808 | bytes 51412992 | tf_op jit(solution)/shard_map/rhit,rtc->rhic/dot_general | solution.py:129
  206.5 0.6 copy-done.12
  207.0 0.6 dynamic-slice.5
  208.3 0.1 constant_dynamic-slice_fusion.1
  208.4 1.0 fusion.24
  209.4 0.1 copy.67
  209.5 14.9 %fusion.1 = f32[128,64]{0,1:T(8,128)S(1)} fusion(f32[1,128,64,1024]{3,1,2,0:T(8,128)} %get-tuple-element.19, f32[128,64]{0,1:T(8,128)S(1)} %reduce_max.38), kind=kLoop, calls=%fused_computation.5 | loop fusion | flops 16769024 | bytes 33619968 | tf_op jit(solution)/shard_map/reduce_sum | solution.py:128
  224.5 0.1 copy.53
  224.6 58.5 %all-reduce = f32[1,128,64]{2,1,0:T(8,128)S(1)} all-reduce(f32[1,128,64]{2,1,0:T(8,128)S(1)} %copy.53), channel_id=7, replica_groups=mesh['seq_0'=4,'seq_1'=4,'batch_0'=4,'batch_1'=2] {'seq_0','seq_1'}, use_global_device_ids=true, to_apply=%region_5.6.clone | all-reduce | flops 8192 | bytes 65536
  283.1 0.1 copy.55
  283.2 0.1 copy.61
  283.4 33.9 %reduce-scatter.3.cloned.1.call-done = f32[1,8,64,512]{3,1,2,0:T(8,128)} async-done(((f32[1,128,64,512]{3,1,2,0:T(8,128)}), f32[1,8,64,512]{3,1,2,0:T(8,128)}) %reduce-scatter.3.cloned.1.call-update) | async-done | bytes 1048592 | tf_op jit(solution)/shard_map/reduce_scatter | solution.py:146
  317.3 1.5 fusion.15
  318.9 0.4 fusion.19
  319.2 0.1 copy.57
  319.4 7.9 %fusion.27 = f32[64,7168]{1,0:T(8,128)S(1)} fusion(bf16[1024,7168]{1,0:T(8,128)(2,1)} %param.25, bf16[8,8,8,128]{3,2,1,0:T(8,128)(2,1)S(1)} %bitcast.377), kind=kOutput, calls=%fused_computation.45 | convolution fusion | flops 939524096 | bytes 16646144 | tf_op jit(solution)/shard_map/dot_general | solution.py:157
  327.2 0.1 convert_add_fusion
  327.4 1.1 add.352
  328.5 1.2 copy-done.2
  329.8 88.2 %all-reduce.3.cloned.1.call-done = f32[64,7168]{1,0:T(8,128)} async-done(((f32[64,7168]{1,0:T(8,128)}), f32[64,7168]{1,0:T(8,128)}) %all-reduce.3.cloned.1.call-update) | async-done | bytes 1835024 | tf_op jit(solution)/shard_map/psum | solution.py:163
  418.0 1.7 multiply_reduce_fusion
  419.7 2.7 multiply_convert_fusion
  423.1 0.1 eq.74
  423.2 0.1 reshape.1086
  423.3 1.6 dynamic-slice_convert_fusion
  425.0 43.8 %all-gather.13.cloned.1.call-done = bf16[512,7168]{1,0:T(8,128)(2,1)} async-done(((bf16[64,7168]{1,0:T(8,128)(2,1)}), bf16[512,7168]{1,0:T(8,128)(2,1)}) %all-gather.13.cloned.1.call-update) | async-done | bytes 7340048 | tf_op jit(solution)/shard_map/all_gather | solution.py:175
  468.8 8.5 %fusion.98 = (f32[512]{0:T(512)S(1)}, f32[512,512]{0,1:T(8,128)S(1)}) fusion(bf16[512,7168]{1,0:T(8,128)(2,1)} %all-gather.13.cloned.1.call-done, bf16[512,7168]{1,0:T(8,128)(2,1)} %param.27), kind=kOutput, calls=%fused_computation.170 | convolution fusion | flops 3758358016 | bytes 15730688 | tf_op jit(solution)/shard_map/rd,vd->rv/dot_general | solution.py:173
  477.3 0.3 copy.58
  477.6 0.2 exponential_reduce_fusion
  477.8 1.6 gather_fusion
  479.5 0.3 select_reduce_fusion
  479.7 9.6 %all-gather.4 = f32[4,3,512]{2,1,0:T(4,128)S(1)} all-gather(f32[1,3,512]{2,1,0:T(4,128)S(1)} %maximum_bitcast_fusion.1), channel_id=2, replica_groups=mesh['seq_0'=4,'seq_1'=4,'batch_0'=4,'batch_1'=2] {'seq_0'}, dimensions={0}, use_global_device_ids=true | all-gather | bytes 30720 | tf_op jit(solution)/shard_map/all_gather | solution.py:43
  489.4 9.5 %all-gather.5 = f32[4,3,512]{2,1,0:T(4,128)S(1)} all-gather(f32[1,3,512]{2,1,0:T(4,128)S(1)} %maximum_bitcast_fusion.2), channel_id=3, replica_groups=mesh['seq_0'=4,'seq_1'=4,'batch_0'=4,'batch_1'=2] {'seq_1'}, dimensions={0}, use_global_device_ids=true | all-gather | bytes 30720 | tf_op jit(solution)/shard_map/all_gather | solution.py:43
  498.9 9.0 %all-gather.6 = f32[4,3,512]{2,1,0:T(4,128)S(1)} all-gather(f32[1,3,512]{2,1,0:T(4,128)S(1)} %maximum_bitcast_fusion.3), channel_id=4, replica_groups=mesh['seq_0'=4,'seq_1'=4,'batch_0'=4,'batch_1'=2] {'batch_0'}, dimensions={0}, use_global_device_ids=true | all-gather | bytes 30720 | tf_op jit(solution)/shard_map/all_gather | solution.py:43
  508.0 10.2 %all-gather.7 = f32[2,3,512]{2,1,0:T(4,128)S(1)} all-gather(f32[1,3,512]{2,1,0:T(4,128)S(1)} %maximum_bitcast_fusion.4), channel_id=5, replica_groups=mesh['seq_0'=4,'seq_1'=4,'batch_0'=4,'batch_1'=2] {'batch_1'}, dimensions={0}, use_global_device_ids=true | all-gather | bytes 18432 | tf_op jit(solution)/shard_map/all_gather | solution.py:43
  518.3 3.5 gather_fusion.1
  521.8 0.1 gather.10
  521.8 0.1 add.384
  521.9 1.1 fusion.89
  (61 shorter events, 0.9 us)
Async XLA Ops:
  7.2 113.3 %copy-start = (bf16[1,1024,512]{2,1,0:T(8,128)(2,1)S(1)}, bf16[1,1024,512]{2,1,0:T(8,128)(2,1)}, u32[]{:S(2)}) copy-start(bf16[1,1024,512]{2,1,0:T(8,128)(2,1)} %param.20) | copy-start | bytes 3145732
  7.2 92.3 %copy-start.5 = (bf16[1,64,512]{2,1,0:T(8,128)(2,1)S(1)}, bf16[1,64,512]{2,1,0:T(8,128)(2,1)}, u32[]{:S(2)}) copy-start(bf16[1,64,512]{2,1,0:T(8,128)(2,1)} %param.22) | copy-start | bytes 196612
  7.2 87.5 %all-gather.11.cloned.1.call-start = ((), (), s32[]{:S(2)}) async-start(), calls=%async_computation.2 | async-start | bytes 11141120 | tf_op jit(solution)/shard_map/all_gather | solution.py:22
  10.8 306.5 %reduce-scatter.3.cloned.1.call-start = ((), (), s32[]{:S(2)}) async-start(), calls=%async_computation.3 | async-start | bytes 17825792 | tf_op jit(solution)/shard_map/reduce_scatter | solution.py:146
  96.5 10.4 %copy-start.8 = (bf16[1,64,64]{2,1,0:T(8,128)(2,1)S(1)}, bf16[1,64,64]{2,1,0:T(8,128)(2,1)}, u32[]{:S(2)}) copy-start(bf16[1,64,64]{2,1,0:T(8,128)(2,1)} %param.23) | copy-start | bytes 24580
  120.5 30.0 %copy-start.3 = (bf16[1,64,128,64]{2,3,1,0:T(8,128)(2,1)S(1)}, bf16[1,64,128,64]{2,3,1,0:T(8,128)(2,1)}, u32[]{:S(2)}) copy-start(bf16[1,64,128,64]{2,3,1,0:T(8,128)(2,1)} %copy.69) | copy-start | bytes 3145732
  120.5 30.0 %copy-start.4 = (bf16[1,1024,64]{1,2,0:T(8,128)(2,1)S(1)}, bf16[1,1024,64]{1,2,0:T(8,128)(2,1)}, u32[]{:S(2)}) copy-start(bf16[1,1024,64]{1,2,0:T(8,128)(2,1)} %param.21) | copy-start | bytes 393220
  206.4 0.7 copy-start.12
  206.4 211.5 %all-reduce.3.cloned.1.call-start = ((), (), s32[]{:S(2)}) async-start(), calls=%async_computation.4 | async-start | bytes 3670016 | tf_op jit(solution)/shard_map/psum | solution.py:163
  209.5 109.3 %copy-start.11 = (bf16[8,512,128]{2,1,0:T(8,128)(2,1)S(1)}, bf16[8,512,128]{2,1,0:T(8,128)(2,1)}, u32[]{:S(2)}) copy-start(bf16[8,512,128]{2,1,0:T(8,128)(2,1)} %param.19) | copy-start | bytes 3145732
  319.3 7.9 %copy-start.6 = (bf16[64,448]{1,0:T(8,128)(2,1)S(1)}, bf16[64,448]{1,0:T(8,128)(2,1)}, u32[]{:S(2)}) copy-start(bf16[64,448]{1,0:T(8,128)(2,1)} %param.24) | copy-start | bytes 172036
  319.3 100.3 %copy-start.7 = (f32[7168]{0:T(1024)S(1)}, f32[7168]{0:T(1024)}, u32[]{:S(2)}) copy-start(f32[7168]{0:T(1024)} %param.26) | copy-start | bytes 86020
  319.4 103.7 %copy-start.9 = (s32[8,64]{1,0:T(8,128)S(1)}, s32[8,64]{1,0:T(8,128)}, u32[]{:S(2)}) copy-start(s32[8,64]{1,0:T(8,128)} %param.29) | copy-start | bytes 6148
  319.4 103.8 %copy-start.10 = (s32[8,64]{1,0:T(8,128)S(1)}, s32[8,64]{1,0:T(8,128)}, u32[]{:S(2)}) copy-start(s32[8,64]{1,0:T(8,128)} %param.28) | copy-start | bytes 6148
  328.5 1.3 copy-start.2
  329.7 139.0 %all-gather.13.cloned.1.call-start = ((), (), s32[]{:S(2)}) async-start(), calls=%async_computation.5 | async-start | bytes 8257536 | tf_op jit(solution)/shard_map/all_gather | solution.py:175
  468.8 54.3 %copy-start.1 = (bf16[1,1024,512]{2,1,0:T(8,128)(2,1)S(1)}, bf16[1,1024,512]{2,1,0:T(8,128)(2,1)}, u32[]{:S(2)}) copy-start(bf16[1,1024,512]{2,1,0:T(8,128)(2,1)} %param.20) | copy-start | bytes 3145732
Sparse Core Ops, SparseCore 0:
  10.9 83.7 all-gather.10
  206.5 110.7 reduce-scatter.2
  329.9 88.0 all-reduce.2
  422.5 46.2 all-gather.12
where the time goes:
time: 530 us
  waiting for transfers between devices  246 us (46%)
  blocking collectives  112 us (21%)
  matrix products  106 us (20%)
  local copies, waits for them, and re-layouts  26 us (5%)
  other arithmetic  23.3 us (4%)
  between operations  16.1 us (3%)
    psum x1, waiting for transfers between devices, body(): stream = lax.psum(branch_term + residual_wide, SEQ)  88.2 us
    all_gather x1, waiting for transfers between devices, sent_together(): lax.all_gather(both, axis, axis=dim, tiled=True)  80.4 us
    unnamed x1, blocking collectives  58.5 us
    all_gather x1, waiting for transfers between devices, body(): lax.all_gather(normed, BATCH, axis=0, tiled=True)  43.8 us
    all_gather x4, blocking collectives, gathered_once(): both, at, found = (lax.all_gather(jnp.concatenate(lines), axis), 0, {})  38.3 us
    reduce_scatter x1, waiting for transfers between devices, body(): lax.psum_scatter(partial_value, SEQ, scatter_dimension=1, tiled=True)  33.9 us
    dot_general x1, matrix products, body(): jnp.einsum('rihc,rtc->rhit', query_all, cache_latent, preferred_element_t...  30 us
    dot_general x1, matrix products, body(): jnp.einsum('rihe,rte->rhit', rope_all, cache_rope, preferred_element_type...  21.9 us
  transfers between devices with their start and end apart: 4, of which 4 were waited for; matrix products, arithmetic and copies ran while one was open for 4% of the time, Pallas kernels for 0%

commit v1 on v0

--- a/solution.py
+++ b/solution.py
@@ -160,7 +160,8 @@
     residual_wide = lax.dynamic_update_slice_in_dim(
         jnp.zeros_like(branch_term), residual.astype(jnp.float32), feature_first, 1
     )
-    stream = lax.psum(branch_term + residual_wide, SEQ)
+    _answer_pages = lambda arr: jnp.sum(jax.lax.all_gather(arr, SEQ), axis=0)
+    stream = _answer_pages(branch_term + residual_wide)
     square = jnp.sum(stream * stream, axis=1)
     normed = (
         stream * lax.rsqrt(square / stream.shape[1] + norm_epsilon)[:, None] * norm_gain

time: 530 us -> 625 us (1.18)
  waiting for transfers between devices: 246 us -> 334 us
  other arithmetic: 23.3 us -> 31.4 us
    all_gather x0 -> x1, waiting for transfers between devices: none -> 176 us  [body(): _answer_pages = lambda arr: jnp.sum(jax.lax.all_gather(arr, SEQ), axis=0)]
    psum x1 -> x0, waiting for transfers between devices: 88.2 us -> none  [body(): stream = lax.psum(branch_term + residual_wide, SEQ)]
    reduce_sum x0 -> x1, other arithmetic: none -> 11 us  [body(): _answer_pages = lambda arr: jnp.sum(jax.lax.all_gather(arr, SEQ), axis=0)]
  transfers between devices with their start and end apart: 4 -> 4, of which waited for: 4 -> 4; matrix products, arithmetic and copies ran while one was open for 4% -> 3% of each run, Pallas kernels for 0% -> 0%
where the time goes in v1:
time: 625 us; the launch traced here: 624 us
  waiting for transfers between devices  334 us (53%)
  blocking collectives  112 us (18%)
  matrix products  106 us (17%)
  other arithmetic  31.4 us (5%)
  local copies, waits for them, and re-layouts  25.1 us (4%)
  between operations  16.1 us (3%)
    all_gather x1, waiting for transfers between devices, body(): _answer_pages = lambda arr: jnp.sum(jax.lax.all_gather(arr, SEQ), axis=0)  176 us
    all_gather x1, waiting for transfers between devices, sent_together(): lax.all_gather(both, axis, axis=dim, tiled=True)  80.4 us
    unnamed x1, blocking collectives  58.5 us
    all_gather x1, waiting for transfers between devices, body(): lax.all_gather(normed, BATCH, axis=0, tiled=True)  43.9 us
    all_gather x4, blocking collectives, gathered_once(): both, at, found = (lax.all_gather(jnp.concatenate(lines), axis), 0, {})  38.3 us
    reduce_scatter x1, waiting for transfers between devices, body(): lax.psum_scatter(partial_value, SEQ, scatter_dimension=1, tiled=True)  33.9 us
    dot_general x1, matrix products, body(): jnp.einsum('rihc,rtc->rhit', query_all, cache_latent, preferred_element_t...  30 us
    dot_general x1, matrix products, body(): jnp.einsum('rihe,rte->rhit', rope_all, cache_rope, preferred_element_type...  21.9 us
  transfers between devices with their start and end apart: 4, of which 4 were waited for; matrix products, arithmetic and copies ran while one was open for 3% of the time, Pallas kernels for 0%

profile of v1, /device:TPU:1, one launch (start us, length us, event | category | flops | bytes accessed | tf_op | source)
XLA Modules:
  0.0 624.3 jit_solution(15148937121159127965)
XLA Ops:
  7.2 1.0 copy.41
  8.2 1.6 fusion.16
  9.9 0.9 maximum_bitcast_fusion
  11.5 0.7 fusion.88
  12.2 0.2 fusion.39
  12.5 0.2 convolution_add_fusion.5
  12.7 0.2 fusion.99
  12.8 0.2 convolution_add_fusion.4
  13.0 0.2 fusion.100
  13.2 0.2 convolution_add_fusion.3
  13.3 0.2 fusion.101
  13.5 0.2 convolution_add_fusion.2
  13.7 0.2 fusion.102
  13.9 0.2 convolution_add_fusion.1
  14.0 0.2 fusion.17
  14.2 0.1 copy.45
  14.3 80.4 %all-gather.12.cloned.1.call-done = bf16[1,64,128,576]{3,1,0,2:T(8,128)(2,1)} async-done(((bf16[1,64,8,576]{3,1,0,2:T(8,128)(2,1)}), bf16[1,64,128,576]{3,1,0,2:T(8,128)(2,1)}) %all-gather.12.cloned.1.call-update) | async-done | bytes 9437200 | tf_op jit(solution)/shard_map/all_gather | solution.py:22
  94.7 1.8 split.9
  96.5 2.9 copy.69
  99.4 7.5 %fusion.10 = f32[64,128,64]{0,2,1:T(8,128)S(1)} fusion(bf16[1,64,512]{2,1,0:T(8,128)(2,1)S(1)} %copy-done.5, bf16[1,64,128,576]{3,1,0,2:T(8,128)(2,1)} %all-gather.12.cloned.1.call-done), kind=kOutput, calls=%fused_computation.11 | convolution fusion | flops 536870912 | bytes 10551296 | tf_op jit(solution)/shard_map/rihc,rjc->rhij/dot_general | solution.py:116
  106.9 5.8 fusion.97
  112.8 7.7 %split.8 = bf16[1,64,128,512]{3,1,0,2:T(8,128)(2,1)} slice(bf16[1,64,128,576]{3,1,0,2:T(8,128)(2,1)} %all-gather.12.cloned.1.call-done), slice={[0:1], [0:64], [0:128], [0:512]} | slice | bytes 16777216 | tf_op jit(solution)/shard_map/split | solution.py:22
  120.5 30.0 %fusion.12 = f32[64,128,1024]{2,1,0:T(8,128)} fusion(bf16[1,64,128,512]{3,1,0,2:T(8,128)(2,1)} %split.8, bf16[1,1024,512]{2,1,0:T(8,128)(2,1)S(1)} %copy-done), kind=kOutput, calls=%fused_computation.14 | convolution fusion | flops 8589934592 | bytes 42991616 | tf_op jit(solution)/shard_map/rihc,rtc->rhit/dot_general | solution.py:107
  150.5 21.9 %fusion.96 = (f32[128,64]{0,1:T(8,128)S(1)}, f32[1,128,64,1024]{3,1,2,0:T(8,128)}) fusion(f32[64,128,1024]{2,1,0:T(8,128)} %fusion.12, bf16[1,1024,64]{1,2,0:T(8,128)(2,1)S(1)} %copy-done.4, bf16[1,64,128,64]{2,3,1,0:T(8,128)(2,1)S(1)} %copy-done.3, pred[1024]{0:T(1024)(128)(4,1)S(1)} %add_compare_fusion), kind=kOutput, calls=%fused_computation.168 | convolution fusion | flops 1107288064 | bytes 68322304 | tf_op jit(solution)/shard_map/rihe,rte->rhit/dot_general | solution.py:110
  172.5 15.1 %all_to_all.5 = f32[16,1,128,64]{2,3,1,0:T(8,128)S(1)} all-to-all(f32[16,1,128,64]{2,3,1,0:T(8,128)S(1)} %broadcast_in_dim.37), channel_id=1, replica_groups=mesh['seq_0'=4,'seq_1'=4,'batch_0'=4,'batch_1'=2] {'seq_0','seq_1'}, dimensions={0} | all-to-all | bytes 1048576 | tf_op jit(solution)/shard_map/all_to_all | solution.py:27
  187.7 18.7 %fusion.7 = f32[1,128,64,512]{3,1,2,0:T(8,128)} fusion(f32[1,128,64,1024]{3,1,2,0:T(8,128)} %get-tuple-element.19, f32[128,64]{0,1:T(8,128)S(1)} %reduce_max.38, bf16[1,1024,512]{2,1,0:T(8,128)(2,1)S(1)} %copy-done), kind=kOutput, calls=%fused_computation.10 | convolution fusion | flops 8606711808 | bytes 51412992 | tf_op jit(solution)/shard_map/rhit,rtc->rhic/dot_general | solution.py:129
  206.5 0.6 copy-done.12
  207.0 0.6 dynamic-slice.5
  208.3 0.1 constant_dynamic-slice_fusion.1
  208.4 1.0 fusion.24
  209.4 0.1 copy.67
  209.5 14.9 %fusion.1 = f32[128,64]{0,1:T(8,128)S(1)} fusion(f32[1,128,64,1024]{3,1,2,0:T(8,128)} %get-tuple-element.19, f32[128,64]{0,1:T(8,128)S(1)} %reduce_max.38), kind=kLoop, calls=%fused_computation.5 | loop fusion | flops 16769024 | bytes 33619968 | tf_op jit(solution)/shard_map/reduce_sum | solution.py:128
  224.5 0.1 copy.53
  224.6 58.5 %all-reduce = f32[1,128,64]{2,1,0:T(8,128)S(1)} all-reduce(f32[1,128,64]{2,1,0:T(8,128)S(1)} %copy.53), channel_id=7, replica_groups=mesh['seq_0'=4,'seq_1'=4,'batch_0'=4,'batch_1'=2] {'seq_0','seq_1'}, use_global_device_ids=true, to_apply=%region_5.6.clone | all-reduce | flops 8192 | bytes 65536
  283.1 0.1 copy.55
  283.2 0.1 copy.61
  283.4 33.9 %reduce-scatter.3.cloned.1.call-done = f32[1,8,64,512]{3,1,2,0:T(8,128)} async-done(((f32[1,128,64,512]{3,1,2,0:T(8,128)}), f32[1,8,64,512]{3,1,2,0:T(8,128)}) %reduce-scatter.3.cloned.1.call-update) | async-done | bytes 1048592 | tf_op jit(solution)/shard_map/reduce_scatter | solution.py:146
  317.3 1.5 fusion.15
  318.9 0.4 fusion.19
  319.2 0.1 copy.57
  319.3 7.9 %fusion.27 = f32[64,7168]{1,0:T(8,128)S(1)} fusion(bf16[1024,7168]{1,0:T(8,128)(2,1)} %param.25, bf16[8,8,8,128]{3,2,1,0:T(8,128)(2,1)S(1)} %bitcast.381), kind=kOutput, calls=%fused_computation.45 | convolution fusion | flops 939524096 | bytes 16646144 | tf_op jit(solution)/shard_map/dot_general | solution.py:157
  327.2 0.1 add_bitcast_fusion
  327.3 1.1 add.350
  328.4 1.3 copy-done.2
  329.8 175.6 %all-gather.14.cloned.1.call-done = f32[16,64,7168]{2,1,0:T(8,128)} async-done(((f32[1,64,7168]{2,1,0:T(8,128)}), f32[16,64,7168]{2,1,0:T(8,128)}) %all-gather.14.cloned.1.call-update) | async-done | bytes 29360144 | tf_op jit(solution)/shard_map/all_gather | solution.py:163
  505.4 11.0 %reduce_sum.73 = f32[64,7168]{1,0:T(8,128)S(1)} reduce(f32[16,64,7168]{2,1,0:T(8,128)} %all-gather.14.cloned.1.call-done, f32[]{:T(128)} %constant.15.clone.1), dimensions={0}, to_apply=%region_7.8 | reduce | flops 6881280 | bytes 31195140 | tf_op jit(solution)/shard_map/reduce_sum | solution.py:163
  516.5 0.2 multiply_reduce_fusion
  516.7 1.2 multiply_convert_fusion
  518.6 0.1 eq.74
  518.7 0.1 reshape.1088
  518.8 0.7 dynamic-slice_convert_fusion
  519.6 43.9 %all-gather.16.cloned.1.call-done = bf16[512,7168]{1,0:T(8,128)(2,1)} async-done(((bf16[64,7168]{1,0:T(8,128)(2,1)}), bf16[512,7168]{1,0:T(8,128)(2,1)}) %all-gather.16.cloned.1.call-update) | async-done | bytes 7340048 | tf_op jit(solution)/shard_map/all_gather | solution.py:176
  563.4 8.5 %fusion.98 = (f32[512]{0:T(512)S(1)}, f32[512,512]{0,1:T(8,128)S(1)}) fusion(bf16[512,7168]{1,0:T(8,128)(2,1)} %all-gather.16.cloned.1.call-done, bf16[512,7168]{1,0:T(8,128)(2,1)} %param.27), kind=kOutput, calls=%fused_computation.170 | convolution fusion | flops 3758358016 | bytes 15730688 | tf_op jit(solution)/shard_map/rd,vd->rv/dot_general | solution.py:174
  572.0 0.3 copy.58
  572.3 0.2 exponential_reduce_fusion
  572.5 1.6 gather_fusion
  574.1 0.3 select_reduce_fusion
  574.4 9.6 %all-gather.4 = f32[4,3,512]{2,1,0:T(4,128)S(1)} all-gather(f32[1,3,512]{2,1,0:T(4,128)S(1)} %maximum_bitcast_fusion.1), channel_id=2, replica_groups=mesh['seq_0'=4,'seq_1'=4,'batch_0'=4,'batch_1'=2] {'seq_0'}, dimensions={0}, use_global_device_ids=true | all-gather | bytes 30720 | tf_op jit(solution)/shard_map/all_gather | solution.py:43
  584.1 9.5 %all-gather.5 = f32[4,3,512]{2,1,0:T(4,128)S(1)} all-gather(f32[1,3,512]{2,1,0:T(4,128)S(1)} %maximum_bitcast_fusion.2), channel_id=3, replica_groups=mesh['seq_0'=4,'seq_1'=4,'batch_0'=4,'batch_1'=2] {'seq_1'}, dimensions={0}, use_global_device_ids=true | all-gather | bytes 30720 | tf_op jit(solution)/shard_map/all_gather | solution.py:43
  593.7 9.0 %all-gather.6 = f32[4,3,512]{2,1,0:T(4,128)S(1)} all-gather(f32[1,3,512]{2,1,0:T(4,128)S(1)} %maximum_bitcast_fusion.3), channel_id=4, replica_groups=mesh['seq_0'=4,'seq_1'=4,'batch_0'=4,'batch_1'=2] {'batch_0'}, dimensions={0}, use_global_device_ids=true | all-gather | bytes 30720 | tf_op jit(solution)/shard_map/all_gather | solution.py:43
  602.7 10.2 %all-gather.7 = f32[2,3,512]{2,1,0:T(4,128)S(1)} all-gather(f32[1,3,512]{2,1,0:T(4,128)S(1)} %maximum_bitcast_fusion.4), channel_id=5, replica_groups=mesh['seq_0'=4,'seq_1'=4,'batch_0'=4,'batch_1'=2] {'batch_1'}, dimensions={0}, use_global_device_ids=true | all-gather | bytes 18432 | tf_op jit(solution)/shard_map/all_gather | solution.py:43
  612.9 3.5 gather_fusion.1
  616.4 0.1 gather.10
  616.6 1.1 fusion.89
  (62 shorter events, 1.0 us)
Async XLA Ops:
  7.2 113.3 %copy-start = (bf16[1,1024,512]{2,1,0:T(8,128)(2,1)S(1)}, bf16[1,1024,512]{2,1,0:T(8,128)(2,1)}, u32[]{:S(2)}) copy-start(bf16[1,1024,512]{2,1,0:T(8,128)(2,1)} %param.20) | copy-start | bytes 3145732
  7.2 92.3 %copy-start.5 = (bf16[1,64,512]{2,1,0:T(8,128)(2,1)S(1)}, bf16[1,64,512]{2,1,0:T(8,128)(2,1)}, u32[]{:S(2)}) copy-start(bf16[1,64,512]{2,1,0:T(8,128)(2,1)} %param.22) | copy-start | bytes 196612
  7.2 87.5 %all-gather.12.cloned.1.call-start = ((), (), s32[]{:S(2)}) async-start(), calls=%async_computation.2 | async-start | bytes 11141120 | tf_op jit(solution)/shard_map/all_gather | solution.py:22
  10.8 306.5 %reduce-scatter.3.cloned.1.call-start = ((), (), s32[]{:S(2)}) async-start(), calls=%async_computation.3 | async-start | bytes 17825792 | tf_op jit(solution)/shard_map/reduce_scatter | solution.py:146
  96.5 10.4 %copy-start.8 = (bf16[1,64,64]{2,1,0:T(8,128)(2,1)S(1)}, bf16[1,64,64]{2,1,0:T(8,128)(2,1)}, u32[]{:S(2)}) copy-start(bf16[1,64,64]{2,1,0:T(8,128)(2,1)} %param.23) | copy-start | bytes 24580
  120.5 30.0 %copy-start.3 = (bf16[1,64,128,64]{2,3,1,0:T(8,128)(2,1)S(1)}, bf16[1,64,128,64]{2,3,1,0:T(8,128)(2,1)}, u32[]{:S(2)}) copy-start(bf16[1,64,128,64]{2,3,1,0:T(8,128)(2,1)} %copy.69) | copy-start | bytes 3145732
  120.5 30.0 %copy-start.4 = (bf16[1,1024,64]{1,2,0:T(8,128)(2,1)S(1)}, bf16[1,1024,64]{1,2,0:T(8,128)(2,1)}, u32[]{:S(2)}) copy-start(bf16[1,1024,64]{1,2,0:T(8,128)(2,1)} %param.21) | copy-start | bytes 393220
  206.4 0.7 copy-start.12
  206.4 299.0 %all-gather.14.cloned.1.call-start = ((), (), s32[]{:S(2)}) async-start(), calls=%async_computation.4 | async-start | bytes 31195136 | tf_op jit(solution)/shard_map/all_gather | solution.py:163
  209.5 109.3 %copy-start.11 = (bf16[8,512,128]{2,1,0:T(8,128)(2,1)S(1)}, bf16[8,512,128]{2,1,0:T(8,128)(2,1)}, u32[]{:S(2)}) copy-start(bf16[8,512,128]{2,1,0:T(8,128)(2,1)} %param.19) | copy-start | bytes 3145732
  319.3 7.9 %copy-start.6 = (bf16[64,448]{1,0:T(8,128)(2,1)S(1)}, bf16[64,448]{1,0:T(8,128)(2,1)}, u32[]{:S(2)}) copy-start(bf16[64,448]{1,0:T(8,128)(2,1)} %param.24) | copy-start | bytes 172036
  328.4 1.3 copy-start.2
  329.7 187.0 %copy-start.7 = (f32[7168]{0:T(1024)S(1)}, f32[7168]{0:T(1024)}, u32[]{:S(2)}) copy-start(f32[7168]{0:T(1024)} %param.26) | copy-start | bytes 86020
  329.7 188.8 %copy-start.9 = (s32[8,64]{1,0:T(8,128)S(1)}, s32[8,64]{1,0:T(8,128)}, u32[]{:S(2)}) copy-start(s32[8,64]{1,0:T(8,128)} %param.29) | copy-start | bytes 6148
  329.7 188.9 %copy-start.10 = (s32[8,64]{1,0:T(8,128)S(1)}, s32[8,64]{1,0:T(8,128)}, u32[]{:S(2)}) copy-start(s32[8,64]{1,0:T(8,128)} %param.28) | copy-start | bytes 6148
  329.8 233.7 %all-gather.16.cloned.1.call-start = ((), (), s32[]{:S(2)}) async-start(), calls=%async_computation.5 | async-start | bytes 8257536 | tf_op jit(solution)/shard_map/all_gather | solution.py:176
  563.4 54.3 %copy-start.1 = (bf16[1,1024,512]{2,1,0:T(8,128)(2,1)S(1)}, bf16[1,1024,512]{2,1,0:T(8,128)(2,1)}, u32[]{:S(2)}) copy-start(bf16[1,1024,512]{2,1,0:T(8,128)(2,1)} %param.20) | copy-start | bytes 3145732
Sparse Core Ops, SparseCore 0:
  10.9 83.7 all-gather.11
  206.5 110.7 reduce-scatter.2
  329.8 175.5 all-gather.13
  518.0 45.3 all-gather.15
